TPU v7x, 256 devices: a whole 4x4x8 slice. The times are simulated.
256 devices in a mesh: seq: 16 (over y, x), fsdp: 16 (over z, core).
Axes of the slice: x: 4, y: 4, z: 8, core: 2. Of those that a mesh axis runs over, the one named last changes fastest.
Arguments:
- kv_cache: bfloat16 [2, 32, 8192, 1280], P(None, 'fsdp', 'seq'), may hold values from -6 to 6
- keep_flags: int32 [32, 8192], P('fsdp', 'seq'), may hold values from 0 to 1, as said below
- block_weights: float32 [32, 8192], P('fsdp', 'seq'), may hold values from 0.05 to 2
- lengths: int32 [32], P('fsdp'), may hold values from 2048 to 8192, as said below
- token_qkv: bfloat16 [32, 3840], P('fsdp'), may hold values from -10 to 10
- stream: bfloat16 [32, 1280], P('fsdp'), may hold values from -0.59765625 to 0.59765625
- w_out: bfloat16 [1280, 1280], P(None, 'fsdp'), may hold values from -0.15625 to 0.15625
- w_up: bfloat16 [1280, 1280], P(None, 'fsdp'), may hold values from -0.15625 to 0.15625
- w_down: bfloat16 [1280, 1280], P(None, 'fsdp'), may hold values from -0.15625 to 0.15625
- w_qkv: bfloat16 [1280, 3840], P(None, 'fsdp'), may hold values from -0.15625 to 0.15625
- mlp_gain: float32 [1280], replicated, may hold values from 0.1 to 1.9
- next_gain: float32 [1280], replicated, may hold values from 0.1 to 1.9
Outputs:
- packed_cache: bfloat16 [2, 32, 8192, 1280], P(None, 'fsdp', 'seq')
- block_summary: bfloat16 [2, 32, 512, 1280], P(None, 'fsdp', 'seq')
- layer_out: bfloat16 [32, 1280], P('fsdp', 'seq')
- next_qkv: bfloat16 [32, 3840], P('fsdp', 'seq')
Inputs may be any that keep to these rules, and one draw needn't show every extreme that they name: `keep_flags`: in every draw one request keeps all 512 positions of one aligned block of 512 positions. `lengths`: in every draw some request has 8192 filled positions.
All inputs are finite; a program needn't handle non-finite values.
Results may differ from a plain program's by a relative error of at most 0.02.
Values may be sent and summed in bfloat16 or wider, within the bound.
A program may use at most 128 MiB of HBM per device.

v0:
```python
import math

import jax
import jax.numpy as jnp
from jax import lax
from jax.sharding import PartitionSpec as P

H = 16
BLK = 16


neg_fill = -1e30


def combined_all(part, axis, combine):
    gathered = jax.tree.map(lambda a: lax.all_gather(a, axis), part)

    def take(source):
        return jax.tree.map(lambda a: lax.dynamic_index_in_dim(a, source, 0, False), gathered)

    return lax.fori_loop(
        1, lax.axis_size(axis), lambda source, state: combine(state, take(source)), take(0)
    )


def normalize(values, gain):
    wide = values.astype(jnp.float32)
    factor = lax.rsqrt(jnp.mean(wide * wide, axis=-1, keepdims=True) + 1e-06)
    return (wide * factor * gain).astype(jnp.bfloat16)


def combine_parts(first, second):
    peak_a, total_a, accum_a = first
    peak_b, total_b, accum_b = second
    peak = jnp.maximum(peak_a, peak_b)
    factor_a = jnp.exp(peak_a - peak)
    factor_b = jnp.exp(peak_b - peak)
    return (
        peak,
        total_a * factor_a + total_b * factor_b,
        accum_a * factor_a[..., None] + accum_b * factor_b[..., None],
    )


def partial_softmax(queries, keys, values, usable, inv_root):
    scores = (
        jnp.einsum("rhe,rnhe->rhn", queries, keys, preferred_element_type=jnp.float32) * inv_root
    )
    scores = jnp.where(usable[:, None, :], scores, neg_fill)
    peak = jnp.max(scores, axis=-1)
    expo = jnp.where(usable[:, None, :], jnp.exp(scores - peak[..., None]), 0.0)
    total = jnp.sum(expo, axis=-1)
    accum = jnp.einsum("rhn,rnhe->rhe", expo, values, preferred_element_type=jnp.float32)
    return (peak, total, accum)


def split_heads(block):
    return block.reshape(block.shape[:-1] + (H, block.shape[-1] // H))


def body(
    kv_cache,
    keep_flags,
    block_weights,
    lengths,
    token_qkv,
    stream,
    w_out,
    w_up,
    w_down,
    w_qkv,
    mlp_gain,
    next_gain,
):
    seq_count = lax.axis_size("seq")
    seq_here = lax.axis_index("seq")
    reqs = kv_cache.shape[1]
    rows = kv_cache.shape[2]
    width = kv_cache.shape[3]
    head_size = width // H
    inv_root = 1.0 / math.sqrt(head_size)
    position = seq_here * rows + jnp.arange(rows, dtype=jnp.int32)
    in_range = position[None, :] < lengths[:, None]
    kept_rows = in_range & (keep_flags == 1)
    drop_rows = in_range & (keep_flags == 0)
    inclusive = jnp.cumsum(kept_rows.astype(jnp.int32), axis=1)
    held = inclusive[:, -1]
    every = lax.all_gather(held[None, :], "seq", axis=0, tiled=True)
    lower = jnp.arange(seq_count, dtype=jnp.int32)[:, None] < seq_here
    before = jnp.sum(jnp.where(lower, every, 0), axis=0)
    blocks = rows // BLK
    drop_weight = jnp.where(drop_rows, block_weights, 0.0).reshape(reqs, blocks, BLK)
    weight_total = jnp.sum(drop_weight, axis=-1)
    drop_count = jnp.sum(drop_rows.reshape(reqs, blocks, BLK).astype(jnp.int32), axis=-1)
    sums = jnp.einsum(
        "rbk,crbkd->crbd",
        drop_weight,
        kv_cache.reshape(2, reqs, blocks, BLK, width),
        preferred_element_type=jnp.float32,
        precision=lax.Precision.HIGHEST,
    )
    block_summary = (sums / jnp.maximum(weight_total, 1.0)[None, :, :, None]).astype(jnp.bfloat16)
    queries = split_heads(token_qkv[:, :width])
    own_keys = split_heads(token_qkv[:, width : 2 * width])
    own_values = split_heads(token_qkv[:, 2 * width :])
    slot = rows // seq_count
    target = jnp.arange(seq_count, dtype=jnp.int32)
    offset = jnp.mod(target[:, None] - before[None, :], seq_count)
    sent = (held[None, :] - offset + seq_count - 1) // seq_count
    wanted = offset[:, :, None] + seq_count * jnp.arange(slot, dtype=jnp.int32)[None, None, :]
    local_rank = inclusive - 1
    wanted_r = jnp.transpose(wanted, (1, 0, 2))
    pick_send = (
        kept_rows[:, None, None, :] & (local_rank[:, None, None, :] == wanted_r[:, :, :, None])
    ).astype(jnp.bfloat16)
    outgoing = jnp.einsum(
        "rtsp,crpd->ctrsd", pick_send, kv_cache, preferred_element_type=jnp.float32
    ).astype(jnp.bfloat16)
    incoming, arrived = (
        lax.all_to_all(outgoing, "seq", split_axis=1, concat_axis=1, tiled=True),
        lax.all_to_all(sent[None], "seq", split_axis=1, concat_axis=1, tiled=True),
    )
    counts_in = arrived[0]
    ends = jnp.cumsum(counts_in, axis=0)
    starts = ends - counts_in
    filled = ends[-1]
    local_rows = jnp.arange(rows, dtype=jnp.int32)
    slot_index = jnp.arange(slot, dtype=jnp.int32)
    starts_r = starts.T
    counts_r = counts_in.T
    valid_slot = slot_index[None, None, :] < counts_r[:, :, None]
    dest_row = starts_r[:, :, None] + slot_index[None, None, :]
    pick_recv = (
        valid_slot[:, None, :, :] & (dest_row[:, None, :, :] == local_rows[None, :, None, None])
    ).astype(jnp.bfloat16)
    packed_cache = jnp.einsum(
        "rlts,ctrsd->crld", pick_recv, incoming, preferred_element_type=jnp.float32
    ).astype(jnp.bfloat16)
    present = local_rows[None, :] < filled[:, None]
    row_part = partial_softmax(
        queries, split_heads(packed_cache[0]), split_heads(packed_cache[1]), present, inv_root
    )
    summary_part = partial_softmax(
        queries,
        split_heads(block_summary[0]),
        split_heads(block_summary[1]),
        drop_count > 0,
        inv_root,
    )
    peak, total, accum = combined_all(combine_parts(row_part, summary_part), "seq", combine_parts)
    own_score = (
        jnp.einsum("rhe,rhe->rh", queries, own_keys, preferred_element_type=jnp.float32) * inv_root
    )
    top_score = jnp.maximum(peak, own_score)
    factor_old = jnp.exp(peak - top_score)
    factor_own = jnp.exp(own_score - top_score)
    attended = (
        accum * factor_old[..., None] + factor_own[..., None] * own_values.astype(jnp.float32)
    ) / (total * factor_old + factor_own)[..., None]
    attended = attended.reshape(reqs, width).astype(jnp.bfloat16)
    fsdp_here = lax.axis_index("fsdp")

    def widen(columns):
        return lax.all_gather(columns, "fsdp", axis=1, tiled=True)

    def own_columns(full, count):
        return lax.dynamic_slice_in_dim(full, fsdp_here * count, count, 1)

    attn_all, stream_all = (
        lax.all_gather(attended, "fsdp", axis=0, tiled=True),
        lax.all_gather(stream, "fsdp", axis=0, tiled=True),
    )
    mid_cols = own_columns(stream_all, w_out.shape[1]).astype(jnp.float32) + jnp.dot(
        attn_all, w_out, preferred_element_type=jnp.float32
    )
    mid = widen(mid_cols.astype(jnp.bfloat16))
    hidden = widen(
        jax.nn.silu(
            jnp.dot(normalize(mid, mlp_gain), w_up, preferred_element_type=jnp.float32)
        ).astype(jnp.bfloat16)
    )
    out_cols = own_columns(mid, w_down.shape[1]).astype(jnp.float32) + jnp.dot(
        hidden, w_down, preferred_element_type=jnp.float32
    )
    layer_all = widen(out_cols.astype(jnp.bfloat16))
    qkv_all = widen(
        jnp.dot(normalize(layer_all, next_gain), w_qkv, preferred_element_type=jnp.float32).astype(
            jnp.bfloat16
        )
    )
    layer_rows = lax.dynamic_slice_in_dim(layer_all, fsdp_here * reqs, reqs, 0)
    qkv_rows = lax.dynamic_slice_in_dim(qkv_all, fsdp_here * reqs, reqs, 0)
    layer_width = width // seq_count
    qkv_width = 3 * width // seq_count
    layer_out = lax.dynamic_slice_in_dim(layer_rows, seq_here * layer_width, layer_width, 1)
    next_qkv = lax.dynamic_slice_in_dim(qkv_rows, seq_here * qkv_width, qkv_width, 1)
    return (packed_cache, block_summary, layer_out, next_qkv)


def solution(mesh):
    placed = (
        P(None, "fsdp", "seq", None),
        P("fsdp", "seq"),
        P("fsdp", "seq"),
        P("fsdp"),
        P("fsdp", None),
        P("fsdp", None),
        P(None, "fsdp"),
        P(None, "fsdp"),
        P(None, "fsdp"),
        P(None, "fsdp"),
        P(),
        P(),
    )
    return jax.shard_map(
        body,
        mesh=mesh,
        in_specs=placed,
        out_specs=(
            P(None, "fsdp", "seq", None),
            P(None, "fsdp", "seq", None),
            P("fsdp", "seq"),
            P("fsdp", "seq"),
        ),
        check_vma=False,
    )
```

profile of v0, /device:TPU:32, one launch (start us, length us, event | category | flops | bytes accessed | tf_op | source)
XLA Modules:
  0.0 287.1 jit_solution(1825323752103344393)
XLA Ops:
  0.7 0.8 fusion.76
  1.5 0.6 reduce-window.6
  2.1 0.2 slice_reduce_fusion
  2.8 1.3 dynamic-slice
  4.8 16.5 %all-reduce = s32[32]{0:T(128)S(1)} all-reduce(s32[32]{0:T(128)S(1)} %bitcast_dynamic-update-slice_fusion), channel_id=2, replica_groups=mesh['seq'=16,'fsdp'=16] {'seq'}, use_global_device_ids=true, to_apply=%add | all-reduce | flops 32 | bytes 256
  21.5 0.7 and_select_fusion
  22.2 3.5 %all-to-all-start.1 = ((s32[1,16,2]{2,0,1:T(1,128)}), s32[1,16,2]{2,0,1:T(1,128)S(1)}, u32[]{:S(2)}, u32[]{:S(2)}) async-start(s32[1,16,2]{2,0,1:T(1,128)} %and_select_fusion), calls=%async_computation.1 | async-start | bytes 16384 | tf_op jit(solution)/shard_map/all_to_all | solution.py:121
  25.9 5.4 %fusion.7 = bf16[2,16,2,32,1280]{4,3,1,0,2:T(8,128)(2,1)S(1)} fusion(s32[2,16,32]{2,1,0:T(8,128)S(1)} %broadcast_add_fusion, s32[2,512]{1,0:T(2,128)S(1)} %broadcast_add_fusion.1, pred[2,512]{1,0:T(4,128)(4,1)S(1)} %get-tuple-element.236, bf16[2,2,512,1280]{3,2,1,0:T(8,128)(2,1)} %param.14), kind=kOutput, calls=%fused_computation.15 | convolution fusion | flops 2688024576 | bytes 10494976 | tf_op jit(solution)/shard_map/rtsp,crpd->ctrsd/dot_general | solution.py:116
  31.3 2.8 copy.45
  34.1 7.3 %all-to-all-start = ((bf16[2,16,2,32,1280]{4,3,0,2,1:T(8,128)(2,1)}), bf16[2,16,2,32,1280]{4,3,0,2,1:T(8,128)(2,1)}, u32[]{:S(2)}, u32[]{:S(2)}) async-start(bf16[2,16,2,32,1280]{4,3,0,2,1:T(8,128)(2,1)} %copy.45), calls=%async_computation | async-start | bytes 10485760 | tf_op jit(solution)/shard_map/all_to_all | solution.py:120
  42.0 4.8 %fusion.5 = f32[2,32,1,2,1280]{4,2,3,1,0:T(1,128)S(1)} fusion(f32[2,32,16,1,1]{2,3,4,1,0:T(1,128)S(1)} %bitcast.193, bf16[2,2,32,16,1280]{4,3,2,1,0:T(8,128)(2,1)} %bitcast.190), kind=kOutput, calls=%fused_computation.13 | convolution fusion | flops 31457280 | bytes 5902336 | tf_op jit(solution)/shard_map/rbk,crbkd->crbd/dot_general | solution.py:95
  46.9 0.7 copy-done.2
  47.6 0.4 reshape_squeeze.13
  48.2 0.4 reshape_squeeze.15
  48.8 18.2 %all-gather.2 = bf16[16,2,1280]{2,1,0:T(2,128)(2,1)S(1)} all-gather(bf16[1,2,1280]{2,1,0:T(2,128)(2,1)S(1)} %bitcast.202), channel_id=1, replica_groups=mesh['seq'=16,'fsdp'=16] {'fsdp'}, dimensions={0}, use_global_device_ids=true | all-gather | bytes 87040 | tf_op jit(solution)/shard_map/all_gather | solution.py:171
  67.1 0.7 fusion.54
  67.8 0.2 fusion.31
  68.1 0.8 fusion.75
  68.9 0.8 fusion.29
  70.2 38.6 %all-to-all-done = bf16[2,16,2,32,1280]{4,3,0,2,1:T(8,128)(2,1)} async-done(((bf16[2,16,2,32,1280]{4,3,0,2,1:T(8,128)(2,1)}), bf16[2,16,2,32,1280]{4,3,0,2,1:T(8,128)(2,1)}, u32[]{:S(2)}, u32[]{:S(2)}) %all-to-all-start) | async-done | bytes 5242912 | tf_op jit(solution)/shard_map/all_to_all | solution.py:120
  108.9 5.7 %fusion.12 = bf16[2,2,1280,512,1]{3,2,1,0,4:T(8,128)(2,1)S(1)} fusion(bf16[2,16,2,32,1280]{4,3,0,2,1:T(8,128)(2,1)} %all-to-all-done, s32[2,16,32]{2,0,1:T(2,128)S(1)} %iota_add_fusion, pred[2,16,32]{2,0,1:T(4,128)(4,1)S(1)} %iota_compare_fusion.1), kind=kOutput, calls=%fused_computation.19 | convolution fusion | flops 2685403136 | bytes 10490880 | tf_op jit(solution)/shard_map/rlts,ctrsd->crld/dot_general | solution.py:136
  114.5 0.3 copy.109
  114.9 0.3 fusion.78
  115.3 1.9 copy-done.1
  117.2 0.4 fusion.81
  117.8 0.7 fusion.51
  118.5 0.6 fusion.64
  119.1 0.7 fusion.52
  119.8 7.9 %copy.55 = bf16[2,2,512,1280]{3,2,1,0:T(8,128)(2,1)} copy(bf16[2,2,512,1280]{2,3,1,0:T(8,128)(2,1)} %bitcast.188) | data formatting | bytes 10485760
  127.7 1.5 fusion.49
  129.3 0.8 multiply_add_fusion
  130.1 23.6 %all-gather.1 = f32[32,16,80]{2,1,0:T(8,128)S(1)} all-gather(f32[2,16,80]{2,1,0:T(8,128)S(1)} %multiply_add_fusion), channel_id=3, replica_groups=mesh['seq'=16,'fsdp'=16] {'seq'}, dimensions={0}, use_global_device_ids=true | all-gather | bytes 174080 | tf_op jit(solution)/shard_map/all_gather | solution.py:16
  153.7 0.7 fusion.69
  154.4 20.5 %all_gather.38 = f32[16,2,16]{2,1,0:T(2,128)S(1)} all-gather(f32[1,2,16]{2,1,0:T(2,128)S(1)} %get-tuple-element.239), channel_id=1, replica_groups=mesh['seq'=16,'fsdp'=16] {'seq'}, dimensions={0}, use_global_device_ids=true | all-gather | bytes 2176 | tf_op jit(solution)/shard_map/all_gather | solution.py:16
  174.9 23.2 %all_gather.37 = f32[16,2,16]{2,1,0:T(2,128)S(1)} all-gather(f32[1,2,16]{2,1,0:T(2,128)S(1)} %get-tuple-element.240), channel_id=1, replica_groups=mesh['seq'=16,'fsdp'=16] {'seq'}, dimensions={0}, use_global_device_ids=true | all-gather | bytes 2176 | tf_op jit(solution)/shard_map/all_gather | solution.py:16
  198.1 1.5 while.19
  199.6 0.7 multiply_add_fusion.1
  200.5 18.1 %all-gather.3 = bf16[16,2,1280]{2,1,0:T(2,128)(2,1)S(1)} all-gather(bf16[1,2,1280]{2,1,0:T(2,128)(2,1)S(1)} %reshape.375), channel_id=1, replica_groups=mesh['seq'=16,'fsdp'=16] {'fsdp'}, dimensions={0}, use_global_device_ids=true | all-gather | bytes 87040 | tf_op jit(solution)/shard_map/all_gather | solution.py:170
  218.8 16.7 %all-gather.4 = bf16[16,80,32]{1,2,0:T(8,128)(2,1)S(1)} all-gather(bf16[1,80,32]{1,2,0:T(8,128)(2,1)S(1)} %fusion.21), channel_id=1, replica_groups=mesh['seq'=16,'fsdp'=16] {'fsdp'}, dimensions={0}, use_global_device_ids=true | all-gather | bytes 87040 | tf_op jit(solution)/shard_map/all_gather | solution.py:164
  235.9 1.2 fusion.57
  237.1 14.8 %all-gather.5 = bf16[16,80,32]{1,2,0:T(8,128)(2,1)S(1)} all-gather(bf16[1,80,32]{1,2,0:T(8,128)(2,1)S(1)} %fusion.57), channel_id=1, replica_groups=mesh['seq'=16,'fsdp'=16] {'fsdp'}, dimensions={0}, use_global_device_ids=true | all-gather | bytes 87040 | tf_op jit(solution)/shard_map/all_gather | solution.py:164
  252.1 1.1 fusion.20
  253.3 16.1 %all-gather.6 = bf16[16,80,32]{1,2,0:T(8,128)(2,1)S(1)} all-gather(bf16[1,80,32]{1,2,0:T(8,128)(2,1)S(1)} %fusion.20), channel_id=1, replica_groups=mesh['seq'=16,'fsdp'=16] {'fsdp'}, dimensions={0}, use_global_device_ids=true | all-gather | bytes 87040 | tf_op jit(solution)/shard_map/all_gather | solution.py:164
  269.8 0.3 fusion.17
  270.1 15.2 %all-gather.7 = bf16[16,240,32]{1,2,0:T(8,128)(2,1)S(1)} all-gather(bf16[1,240,32]{1,2,0:T(8,128)(2,1)S(1)} %fusion.17), channel_id=1, replica_groups=mesh['seq'=16,'fsdp'=16] {'fsdp'}, dimensions={0}, use_global_device_ids=true | all-gather | bytes 261120 | tf_op jit(solution)/shard_map/all_gather | solution.py:164
  285.4 0.4 reshape.384
  285.8 0.6 dynamic-slice_bitcast_fusion.1
  286.4 0.6 dynamic-slice_bitcast_fusion
  (112 shorter events, 5.6 us)
Async XLA Ops:
  0.6 269.1 %copy-start = (bf16[1280,240]{0,1:T(8,128)(2,1)S(1)}, bf16[1280,240]{0,1:T(8,128)(2,1)}, u32[]{:S(2)}) copy-start(bf16[1280,240]{0,1:T(8,128)(2,1)} %param.23) | copy-start | bytes 1843204
  22.2 11.9 %all-to-all-start.1 = ((s32[1,16,2]{2,0,1:T(1,128)}), s32[1,16,2]{2,0,1:T(1,128)S(1)}, u32[]{:S(2)}, u32[]{:S(2)}) async-start(s32[1,16,2]{2,0,1:T(1,128)} %and_select_fusion), calls=%async_computation.1 | async-start | bytes 16384 | tf_op jit(solution)/shard_map/all_to_all | solution.py:121
  34.1 7.4 %copy-start.10 = (f32[2,512]{1,0:T(2,128)S(1)}, f32[2,512]{1,0:T(2,128)}, u32[]{:S(2)}) copy-start(f32[2,512]{1,0:T(2,128)} %param.16) | copy-start | bytes 12292
  34.1 7.5 %copy-start.7 = (bf16[2,3840]{1,0:T(2,128)(2,1)S(1)}, bf16[2,3840]{1,0:T(2,128)(2,1)}, u32[]{:S(2)}) copy-start(bf16[2,3840]{1,0:T(2,128)(2,1)} %param.18) | copy-start | bytes 46084
  34.1 74.7 %all-to-all-start = ((bf16[2,16,2,32,1280]{4,3,0,2,1:T(8,128)(2,1)}), bf16[2,16,2,32,1280]{4,3,0,2,1:T(8,128)(2,1)}, u32[]{:S(2)}, u32[]{:S(2)}) async-start(bf16[2,16,2,32,1280]{4,3,0,2,1:T(8,128)(2,1)} %copy.45), calls=%async_computation | async-start | bytes 10485760 | tf_op jit(solution)/shard_map/all_to_all | solution.py:120
  41.5 7.3 %copy-start.9 = (bf16[2,1280]{1,0:T(2,128)(2,1)S(1)}, bf16[2,1280]{1,0:T(2,128)(2,1)}, u32[]{:S(2)}) copy-start(bf16[2,1280]{1,0:T(2,128)(2,1)} %param.19) | copy-start | bytes 15364
  46.9 0.7 copy-start.2
  68.1 46.4 %copy-start.4 = (f32[2,16]{1,0:T(2,128)}, f32[2,16]{1,0:T(2,128)S(1)}, u32[]{:S(2)}) copy-start(f32[2,16]{1,0:T(2,128)S(1)} %fusion.60) | copy-start | bytes 388
  114.9 2.3 copy-start.1
  114.9 3.5 %copy-start.5 = (f32[2,16]{1,0:T(2,128)S(1)}, f32[2,16]{1,0:T(2,128)}, u32[]{:S(2)}) copy-start(f32[2,16]{1,0:T(2,128)} %copy-done.4) | copy-start | bytes 388
  119.8 33.9 %copy-start.6 = (f32[2,16]{1,0:T(2,128)S(1)}, f32[2,16]{1,0:T(2,128)}, u32[]{:S(2)}) copy-start(f32[2,16]{1,0:T(2,128)} %copy-done.4) | copy-start | bytes 388
  119.8 98.8 %copy-start.3 = (bf16[1280,80]{0,1:T(8,128)(2,1)S(1)}, bf16[1280,80]{0,1:T(8,128)(2,1)}, u32[]{:S(2)}) copy-start(bf16[1280,80]{0,1:T(8,128)(2,1)} %param.20) | copy-start | bytes 614404
  127.7 142.1 %copy-start.8 = (f32[1280]{0:T(1024)S(1)}, f32[1280]{0:T(1024)}, u32[]{:S(2)}) copy-start(f32[1280]{0:T(1024)} %param.25) | copy-start | bytes 15364
where the time goes:
time: 291 us; the launch traced here: 287 us
  blocking collectives  183 us (63%)
  waiting for transfers between devices  38.6 us (13%)
  matrix products  21.6 us (7%)
  local copies, waits for them, and re-layouts  20.2 us (7%)
  other arithmetic  11 us (4%)
  starting transfers between devices  10.8 us (4%)
    all_gather x3, blocking collectives, combined_all(): gathered = jax.tree.map(lambda a: lax.all_gather(a, axis), part)  67.3 us
    all_gather x4, blocking collectives, widen(): return lax.all_gather(columns, 'fsdp', axis=1, tiled=True)  62.9 us
    all_to_all x1, waiting for transfers between devices, body(): lax.all_to_all(outgoing, 'seq', split_axis=1, concat_axis=1, tiled=True)  38.6 us
    all_gather x1, blocking collectives, body(): lax.all_gather(stream, 'fsdp', axis=0, tiled=True)  18.2 us
    all_gather x1, blocking collectives, body(): lax.all_gather(attended, 'fsdp', axis=0, tiled=True)  18.1 us
    unnamed x1, blocking collectives  16.5 us
    unnamed x35, local copies, waits for them, and re-layouts  13.1 us
    all_to_all x1, starting transfers between devices, body(): lax.all_to_all(outgoing, 'seq', split_axis=1, concat_axis=1, tiled=True)  7.34 us
  transfers between devices with their start and end apart: 2, of which 1 were waited for; matrix products, arithmetic and copies ran while one was open for 6% of the time, Pallas kernels for 0%

commit v1 on v0

--- a/solution.py
+++ b/solution.py
@@ -10,17 +10,6 @@
 
 
 neg_fill = -1e30
-
-
-def combined_all(part, axis, combine):
-    gathered = jax.tree.map(lambda a: lax.all_gather(a, axis), part)
-
-    def take(source):
-        return jax.tree.map(lambda a: lax.dynamic_index_in_dim(a, source, 0, False), gathered)
-
-    return lax.fori_loop(
-        1, lax.axis_size(axis), lambda source, state: combine(state, take(source)), take(0)
-    )
 
 
 def normalize(values, gain):
@@ -85,8 +74,9 @@
     drop_rows = in_range & (keep_flags == 0)
     inclusive = jnp.cumsum(kept_rows.astype(jnp.int32), axis=1)
     held = inclusive[:, -1]
-    every = lax.all_gather(held[None, :], "seq", axis=0, tiled=True)
-    lower = jnp.arange(seq_count, dtype=jnp.int32)[:, None] < seq_here
+    every = lax.all_gather(held, "seq", axis=0)
+    source = jnp.arange(seq_count, dtype=jnp.int32)
+    lower = source[:, None] < seq_here
     before = jnp.sum(jnp.where(lower, every, 0), axis=0)
     blocks = rows // BLK
     drop_weight = jnp.where(drop_rows, block_weights, 0.0).reshape(reqs, blocks, BLK)
@@ -103,10 +93,10 @@
     queries = split_heads(token_qkv[:, :width])
     own_keys = split_heads(token_qkv[:, width : 2 * width])
     own_values = split_heads(token_qkv[:, 2 * width :])
+
     slot = rows // seq_count
     target = jnp.arange(seq_count, dtype=jnp.int32)
     offset = jnp.mod(target[:, None] - before[None, :], seq_count)
-    sent = (held[None, :] - offset + seq_count - 1) // seq_count
     wanted = offset[:, :, None] + seq_count * jnp.arange(slot, dtype=jnp.int32)[None, None, :]
     local_rank = inclusive - 1
     wanted_r = jnp.transpose(wanted, (1, 0, 2))
@@ -116,14 +106,13 @@
     outgoing = jnp.einsum(
         "rtsp,crpd->ctrsd", pick_send, kv_cache, preferred_element_type=jnp.float32
     ).astype(jnp.bfloat16)
-    incoming, arrived = (
-        lax.all_to_all(outgoing, "seq", split_axis=1, concat_axis=1, tiled=True),
-        lax.all_to_all(sent[None], "seq", split_axis=1, concat_axis=1, tiled=True),
-    )
-    counts_in = arrived[0]
+    incoming = lax.all_to_all(outgoing, "seq", split_axis=1, concat_axis=1, tiled=True)
+    before_all = jnp.sum(jnp.where(source[:, None] > source[None, :], 1, 0)[:, :, None]
+                         * every[None, :, :], axis=1)
+    offset_in = jnp.mod(seq_here - before_all, seq_count)
+    counts_in = jnp.maximum((every - offset_in + seq_count - 1) // seq_count, 0)
     ends = jnp.cumsum(counts_in, axis=0)
     starts = ends - counts_in
-    filled = ends[-1]
     local_rows = jnp.arange(rows, dtype=jnp.int32)
     slot_index = jnp.arange(slot, dtype=jnp.int32)
     starts_r = starts.T
@@ -136,9 +125,9 @@
     packed_cache = jnp.einsum(
         "rlts,ctrsd->crld", pick_recv, incoming, preferred_element_type=jnp.float32
     ).astype(jnp.bfloat16)
-    present = local_rows[None, :] < filled[:, None]
+
     row_part = partial_softmax(
-        queries, split_heads(packed_cache[0]), split_heads(packed_cache[1]), present, inv_root
+        queries, split_heads(kv_cache[0]), split_heads(kv_cache[1]), kept_rows, inv_root
     )
     summary_part = partial_softmax(
         queries,
@@ -147,7 +136,15 @@
         drop_count > 0,
         inv_root,
     )
-    peak, total, accum = combined_all(combine_parts(row_part, summary_part), "seq", combine_parts)
+    peak, total, accum = combine_parts(row_part, summary_part)
+    packed_parts = jnp.concatenate([peak[..., None], total[..., None], accum], axis=-1)
+    gathered = lax.all_gather(packed_parts, "seq", axis=0)
+    peak_all = gathered[..., 0]
+    top = jnp.max(peak_all, axis=0)
+    scale = jnp.exp(peak_all - top[None])
+    total = jnp.sum(gathered[..., 1] * scale, axis=0)
+    accum = jnp.sum(gathered[..., 2:] * scale[..., None], axis=0)
+    peak = top
     own_score = (
         jnp.einsum("rhe,rhe->rh", queries, own_keys, preferred_element_type=jnp.float32) * inv_root
     )
@@ -166,10 +163,9 @@
     def own_columns(full, count):
         return lax.dynamic_slice_in_dim(full, fsdp_here * count, count, 1)
 
-    attn_all, stream_all = (
-        lax.all_gather(attended, "fsdp", axis=0, tiled=True),
-        lax.all_gather(stream, "fsdp", axis=0, tiled=True),
-    )
+    both = lax.all_gather(jnp.concatenate([attended, stream], axis=1), "fsdp", axis=0, tiled=True)
+    attn_all = both[:, :width]
+    stream_all = both[:, width:]
     mid_cols = own_columns(stream_all, w_out.shape[1]).astype(jnp.float32) + jnp.dot(
         attn_all, w_out, preferred_element_type=jnp.float32
     )

time: 291 us -> 228 us (0.78)
  waiting for transfers between devices: 38.6 us -> 0.01 us
  blocking collectives: 183 us -> 150 us
  local copies, waits for them, and re-layouts: 20.2 us -> 36.8 us
  starting transfers between devices: 10.8 us -> 4.7 us
  other arithmetic: 11 us -> 7.39 us
    all_to_all x1, waiting for transfers between devices: 38.6 us -> 0.01 us  [body(): lax.all_to_all(outgoing, 'seq', split_axis=1, concat_axis=1, tiled=True)]
    all_gather x5 -> x2, blocking collectives: 104 us -> 70.5 us  [the longest x1 52.2 us: body(): gathered = lax.all_gather(packed_parts, 'seq', axis=0)]
    unnamed x35 -> x36, local copies, waits for them, and re-layouts: 13.1 us -> 18.4 us
    slice x2 -> x5, local copies, waits for them, and re-layouts: 0.56 us -> 5.45 us  [the longest x1 4.39 us: body(): kv_cache[0]]
    all_to_all x1 -> x0, starting transfers between devices: 3.47 us -> none  [body(): lax.all_to_all(sent[None], 'seq', split_axis=1, concat_axis=1, tiled=True)]
  transfers between devices with their start and end apart: 2 -> 1, of which waited for: 1 -> 0; matrix products, arithmetic and copies ran while one was open for 6% -> 17% of each run, Pallas kernels for 0% -> 0%
where the time goes in v1:
time: 228 us; the launch traced here: 224 us
  blocking collectives  150 us (66%)
  local copies, waits for them, and re-layouts  36.8 us (16%)
  matrix products  23.6 us (10%)
  other arithmetic  7.39 us (3%)
  starting transfers between devices  4.7 us (2%)
    all_gather x4, blocking collectives, widen(): return lax.all_gather(columns, 'fsdp', axis=1, tiled=True)  63.1 us
    all_gather x1, blocking collectives, body(): gathered = lax.all_gather(packed_parts, 'seq', axis=0)  52.2 us
    unnamed x36, local copies, waits for them, and re-layouts  18.4 us
    all_gather x1, blocking collectives, body(): lax.all_gather(jnp.concatenate([attended, stream], axis=1), 'fsdp', axis=...  18.3 us
    unnamed x1, blocking collectives  16.5 us
    dot_general x1, matrix products, body(): jnp.einsum('rlts,ctrsd->crld', pick_recv, incoming, preferred_element_typ...  5.68 us
    dot_general x1, matrix products, body(): jnp.einsum('rtsp,crpd->ctrsd', pick_send, kv_cache, preferred_element_typ...  5.41 us
    dot_general x1, matrix products, body(): jnp.einsum('rbk,crbkd->crbd', drop_weight, kv_cache.reshape(2, reqs, bloc...  4.77 us
  transfers between devices with their start and end apart: 1, of which 0 were waited for; matrix products, arithmetic and copies ran while one was open for 17% of the time, Pallas kernels for 0%

profile of v1, /device:TPU:32, one launch (start us, length us, event | category | flops | bytes accessed | tf_op | source)
XLA Modules:
  0.0 224.3 jit_solution(8476772941093766490)
XLA Ops:
  0.7 0.8 fusion.83
  1.5 0.6 reduce-window.6
  2.2 0.2 slice_reduce_fusion
  2.4 0.2 reduce-window.9
  2.8 1.3 dynamic-slice
  4.8 16.5 %all-reduce = s32[32]{0:T(128)S(1)} all-reduce(s32[32]{0:T(128)S(1)} %bitcast_dynamic-update-slice_fusion), channel_id=2, replica_groups=mesh['seq'=16,'fsdp'=16] {'seq'}, use_global_device_ids=true, to_apply=%add | all-reduce | flops 32 | bytes 256
  22.0 5.4 %fusion.6 = bf16[2,16,2,32,1280]{4,3,1,0,2:T(8,128)(2,1)S(1)} fusion(s32[2,16,32]{2,1,0:T(8,128)S(1)} %broadcast_add_fusion, s32[2,512]{1,0:T(2,128)S(1)} %broadcast_add_fusion.1, pred[2,512]{1,0:T(4,128)(4,1)S(1)} %get-tuple-element.53, bf16[2,2,512,1280]{3,2,1,0:T(8,128)(2,1)} %param.12), kind=kOutput, calls=%fused_computation.8 | convolution fusion | flops 2688024576 | bytes 10494976 | tf_op jit(solution)/shard_map/rtsp,crpd->ctrsd/dot_general | solution.py:106
  27.4 2.8 %copy.107 = bf16[2,16,2,32,1280]{4,3,0,2,1:T(8,128)(2,1)} copy(bf16[2,16,2,32,1280]{4,3,1,0,2:T(8,128)(2,1)S(1)} %fusion.6) | data formatting | bytes 10485760 | tf_op jit(solution)/shard_map/convert_element_type | solution.py:108
  30.3 4.7 %all-to-all-start = ((bf16[2,16,2,32,1280]{4,3,0,2,1:T(8,128)(2,1)}), bf16[2,16,2,32,1280]{4,3,0,2,1:T(8,128)(2,1)}, u32[]{:S(2)}, u32[]{:S(2)}) async-start(bf16[2,16,2,32,1280]{4,3,0,2,1:T(8,128)(2,1)} %copy.107), calls=%async_computation | async-start | bytes 10485760 | tf_op jit(solution)/shard_map/all_to_all | solution.py:109
  35.2 4.4 %fusion.85 = (bf16[1,2,512,1280]{3,2,1,0:T(8,128)(2,1)}, bf16[1,2,512,1280]{3,2,1,0:T(8,128)(2,1)S(1)}) fusion(bf16[2,2,512,1280]{3,2,1,0:T(8,128)(2,1)} %param.12), kind=kLoop, calls=%fused_computation.145 | loop fusion | bytes 10485760 | tf_op jit(solution)/shard_map/slice | solution.py:130
  39.6 0.6 fusion.87
  40.2 4.4 %copy.146 = bf16[1,2,512,1280]{2,3,1,0:T(8,128)(2,1)} copy(bf16[1,2,512,1280]{3,2,1,0:T(8,128)(2,1)} %get-tuple-element.41) | data formatting | bytes 5242880
  44.7 2.2 fusion.88
  47.1 0.8 fusion.52
  47.9 4.8 %fusion.2 = f32[2,32,1,2,1280]{4,2,3,1,0:T(1,128)S(1)} fusion(f32[2,32,16,1,1]{2,3,4,1,0:T(1,128)S(1)} %bitcast.177, bf16[2,2,32,16,1280]{4,3,2,1,0:T(8,128)(2,1)} %bitcast.171), kind=kOutput, calls=%fused_computation.4 | convolution fusion | flops 31457280 | bytes 5902336 | tf_op jit(solution)/shard_map/rbk,crbkd->crbd/dot_general | solution.py:85
  52.8 0.7 copy-done.1
  53.6 0.7 fusion.86
  54.3 2.0 reshape_squeeze.13
  56.3 1.2 fusion.30
  57.8 1.3 fusion.82
  59.0 1.1 reshape_squeeze.15
  60.1 2.6 %copy.147 = bf16[1,2,512,1280]{2,3,1,0:T(8,128)(2,1)} copy(bf16[1,2,512,1280]{3,2,1,0:T(8,128)(2,1)S(1)} %get-tuple-element.42) | data formatting | bytes 5242880
  62.8 1.0 fusion.28
  63.8 2.5 %fusion.49 = f32[2,16,1,80]{3,2,1,0:T(1,128)S(1)} fusion(bf16[2,512,16,80]{1,3,2,0:T(8,128)(2,1)} %bitcast.176, bf16[2,16,512,1]{2,1,0,3:T(8,128)(2,1)S(1)} %fusion.51), kind=kOutput, calls=%fused_computation.57 | convolution fusion | flops 2621440 | bytes 2664448 | tf_op jit(solution)/shard_map/rhn,rnhe->rhe/dot_general | solution.py:42
  66.3 0.7 bitcast_maximum_fusion
  67.5 52.2 %all-gather.1 = f32[32,16,82]{2,1,0:T(8,128)S(1)} all-gather(f32[2,16,82]{2,1,0:T(8,128)S(1)} %pad_maximum_fusion), channel_id=3, replica_groups=mesh['seq'=16,'fsdp'=16] {'seq'}, dimensions={0}, use_global_device_ids=true | all-gather | bytes 178432 | tf_op jit(solution)/shard_map/all_gather | solution.py:141
  119.8 0.3 copy.148
  120.1 0.2 copy.116
  120.4 0.8 reshape.215
  121.3 0.2 fusion.27
  122.0 0.7 fusion.64
  122.8 18.3 %all-gather.2 = bf16[16,2,2560]{2,1,0:T(2,128)(2,1)S(1)} all-gather(bf16[1,2,2560]{2,1,0:T(2,128)(2,1)S(1)} %maximum_bitcast_fusion), channel_id=1, replica_groups=mesh['seq'=16,'fsdp'=16] {'fsdp'}, dimensions={0}, use_global_device_ids=true | all-gather | bytes 174080 | tf_op jit(solution)/shard_map/all_gather | solution.py:166
  141.1 0.2 fusion.19
  141.3 16.7 %all-gather.3 = bf16[16,80,32]{1,2,0:T(8,128)(2,1)S(1)} all-gather(bf16[1,80,32]{1,2,0:T(8,128)(2,1)S(1)} %fusion.19), channel_id=1, replica_groups=mesh['seq'=16,'fsdp'=16] {'fsdp'}, dimensions={0}, use_global_device_ids=true | all-gather | bytes 87040 | tf_op jit(solution)/shard_map/all_gather | solution.py:161
  158.1 0.2 reshape.226
  158.4 0.3 fusion.60
  158.7 15.0 %all-gather.4 = bf16[16,80,32]{1,2,0:T(8,128)(2,1)S(1)} all-gather(bf16[1,80,32]{1,2,0:T(8,128)(2,1)S(1)} %fusion.60), channel_id=1, replica_groups=mesh['seq'=16,'fsdp'=16] {'fsdp'}, dimensions={0}, use_global_device_ids=true | all-gather | bytes 87040 | tf_op jit(solution)/shard_map/all_gather | solution.py:161
  173.7 0.2 reshape.228
  173.9 0.2 fusion.18
  174.1 16.1 %all-gather.5 = bf16[16,80,32]{1,2,0:T(8,128)(2,1)S(1)} all-gather(bf16[1,80,32]{1,2,0:T(8,128)(2,1)S(1)} %fusion.18), channel_id=1, replica_groups=mesh['seq'=16,'fsdp'=16] {'fsdp'}, dimensions={0}, use_global_device_ids=true | all-gather | bytes 87040 | tf_op jit(solution)/shard_map/all_gather | solution.py:161
  190.6 0.3 fusion.15
  190.9 15.2 %all-gather.6 = bf16[16,240,32]{1,2,0:T(8,128)(2,1)S(1)} all-gather(bf16[1,240,32]{1,2,0:T(8,128)(2,1)S(1)} %fusion.15), channel_id=1, replica_groups=mesh['seq'=16,'fsdp'=16] {'fsdp'}, dimensions={0}, use_global_device_ids=true | all-gather | bytes 261120 | tf_op jit(solution)/shard_map/all_gather | solution.py:161
  206.3 0.4 reshape.232
  206.7 0.6 dynamic-slice_bitcast_fusion.1
  207.3 0.6 dynamic-slice_bitcast_fusion
  208.1 5.7 %fusion.4 = bf16[2,2,1280,512,1]{3,2,0,1,4:T(8,128)(2,1)S(1)} fusion(bf16[2,16,2,32,1280]{4,3,0,2,1:T(8,128)(2,1)} %all-to-all-done, s32[2,16,32]{2,0,1:T(2,128)S(1)} %iota_add_fusion, pred[2,16,32]{2,0,1:T(4,128)(4,1)S(1)} %iota_compare_fusion.1), kind=kOutput, calls=%fused_computation.6 | convolution fusion | flops 2685403136 | bytes 10490880 | tf_op jit(solution)/shard_map/rlts,ctrsd->crld/dot_general | solution.py:125
  213.8 2.6 %copy.181 = bf16[2,2,1280,512,1]{3,2,1,0,4:T(8,128)(2,1)} copy(bf16[2,2,1280,512,1]{3,2,0,1,4:T(8,128)(2,1)S(1)} %fusion.4) | data formatting | bytes 10485760 | tf_op jit(solution)/shard_map/rlts,ctrsd->crld/dot_general | solution.py:125
  216.5 7.9 %copy.121 = bf16[2,2,512,1280]{3,2,1,0:T(8,128)(2,1)} copy(bf16[2,2,512,1280]{2,3,0,1:T(8,128)(2,1)} %bitcast.172) | data formatting | bytes 10485760
  (88 shorter events, 4.3 us)
Async XLA Ops:
  0.6 190.0 %copy-start = (bf16[1280,240]{0,1:T(8,128)(2,1)S(1)}, bf16[1280,240]{0,1:T(8,128)(2,1)}, u32[]{:S(2)}) copy-start(bf16[1280,240]{0,1:T(8,128)(2,1)} %param.21) | copy-start | bytes 1843204
  30.3 4.7 %copy-start.8 = (f32[2,512]{1,0:T(2,128)S(1)}, f32[2,512]{1,0:T(2,128)}, u32[]{:S(2)}) copy-start(f32[2,512]{1,0:T(2,128)} %param.14) | copy-start | bytes 12292
  30.3 177.9 %all-to-all-start = ((bf16[2,16,2,32,1280]{4,3,0,2,1:T(8,128)(2,1)}), bf16[2,16,2,32,1280]{4,3,0,2,1:T(8,128)(2,1)}, u32[]{:S(2)}, u32[]{:S(2)}) async-start(bf16[2,16,2,32,1280]{4,3,0,2,1:T(8,128)(2,1)} %copy.107), calls=%async_computation | async-start | bytes 10485760 | tf_op jit(solution)/shard_map/all_to_all | solution.py:109
  35.2 4.4 %copy-start.5 = (bf16[2,3840]{1,0:T(2,128)(2,1)S(1)}, bf16[2,3840]{1,0:T(2,128)(2,1)}, u32[]{:S(2)}) copy-start(bf16[2,3840]{1,0:T(2,128)(2,1)} %param.16) | copy-start | bytes 46084
  52.8 0.7 copy-start.1
  60.1 2.7 %copy-start.2 = (bf16[2,32,16,80]{3,2,1,0:T(8,128)(2,1)S(1)}, bf16[2,32,16,80]{3,2,1,0:T(8,128)(2,1)}, u32[]{:S(2)}) copy-start(bf16[2,32,16,80]{3,2,1,0:T(8,128)(2,1)} %reshape_squeeze.15) | copy-start | bytes 491524
  62.7 60.0 %copy-start.7 = (bf16[2,1280]{1,0:T(2,128)(2,1)S(1)}, bf16[2,1280]{1,0:T(2,128)(2,1)}, u32[]{:S(2)}) copy-start(bf16[2,1280]{1,0:T(2,128)(2,1)} %param.17) | copy-start | bytes 15364
  62.7 78.4 %copy-start.3 = (bf16[1280,80]{0,1:T(8,128)(2,1)S(1)}, bf16[1280,80]{0,1:T(8,128)(2,1)}, u32[]{:S(2)}) copy-start(bf16[1280,80]{0,1:T(8,128)(2,1)} %param.18) | copy-start | bytes 614404
  62.7 95.6 %copy-start.9 = (bf16[1280,80]{0,1:T(8,128)(2,1)S(1)}, bf16[1280,80]{0,1:T(8,128)(2,1)}, u32[]{:S(2)}) copy-start(bf16[1280,80]{0,1:T(8,128)(2,1)} %param.19) | copy-start | bytes 614404
  62.8 95.7 %copy-start.10 = (f32[1280]{0:T(1024)S(1)}, f32[1280]{0:T(1024)}, u32[]{:S(2)}) copy-start(f32[1280]{0:T(1024)} %param.22) | copy-start | bytes 15364
  62.8 111.2 %copy-start.4 = (bf16[1280,80]{0,1:T(8,128)(2,1)S(1)}, bf16[1280,80]{0,1:T(8,128)(2,1)}, u32[]{:S(2)}) copy-start(bf16[1280,80]{0,1:T(8,128)(2,1)} %param.20) | copy-start | bytes 614404
  62.8 127.9 %copy-start.6 = (f32[1280]{0:T(1024)S(1)}, f32[1280]{0:T(1024)}, u32[]{:S(2)}) copy-start(f32[1280]{0:T(1024)} %param.23) | copy-start | bytes 15364
